TPU v7x, 32 devices: a whole 2x2x4 slice. The times are simulated.
32 devices in a mesh: groups: 2 (over y), seq: 16 (over z, x, core).
Axes of the slice: x: 2, y: 2, z: 4, core: 2. Of those that a mesh axis runs over, the one named last changes fastest.
Arguments:
- key_values: bfloat16 [3, 2048, 8192], P(None, 'seq', 'groups'), parts along dimension 2, may hold values from -14 to 14, as said below
- bases: bfloat16 [3, 2, 1024, 256], replicated, may hold values from -0.1875 to 0.1875
- owner_slots: int32 [3, 64], P(None, ('groups', 'seq')), parts along dimension 1, may hold values from 0 to 15, as said below
Outputs:
- received: bfloat16 [512, 512, 128], P(('groups', 'seq')), parts along dimension 0
- grams: float32 [6, 2, 256, 256], P('groups'), parts along dimension 0
- energies: float32 [6, 2, 1024], P('groups'), parts along dimension 0
There are 2 independent parts, one for each index of `groups`. A program takes and returns all parts, laid end to end along the dimension named above; an argument that names none is the same for every part. Nothing has to cross between parts.
Inputs may be any that keep to these rules, and one draw needn't show every extreme that they name: key_values are finite real values within the range. `owner_slots`: block j of a layer belongs to device j // 2 of seq; the 6 values of one device's blocks over all layers are distinct, so an owner's slot is written at most once; some owner has all 16 slots filled.
All inputs are finite; a program needn't handle non-finite values.
Results may differ from a plain program's by a relative error of at most 0.001.
Values may be sent and summed in bfloat16 or wider, within the bound.
A program may use at most 128 MiB of HBM per device.

v0:
```python
import jax
import jax.numpy as jnp
from jax import lax
from jax.sharding import PartitionSpec as P

REACH = 8
OWNER_SLOT_LIMIT = 2
CAP = 16


def from_behind(block, axis, distance):
    devices = range(lax.axis_size(axis))
    route = [((i - distance) % len(devices), i) for i in devices]
    return lax.ppermute(block, axis, route)


def per_device(key_values, bases, owner_slots):
    dev_count = lax.axis_size("seq")
    layers = key_values.shape[0]
    width = bases.shape[2]
    rank = bases.shape[3]
    tok_dev = key_values.shape[2] // dev_count
    tokens = tok_dev * dev_count
    blk_dev = owner_slots.shape[1]
    blk_rows = tok_dev // blk_dev
    whole = lax.all_to_all(key_values, "seq", split_axis=2, concat_axis=1, tiled=True)
    gram_list = []
    energy_list = []
    block_list = []
    for layer_idx in range(layers):
        slab_rows = whole[layer_idx]
        slab_rows = slab_rows.reshape(2, width, tok_dev)
        basis = bases[layer_idx]
        coeff = jnp.einsum(
            "scr,sct->srt", basis, slab_rows, preferred_element_type=jnp.float32
        ).astype(jnp.bfloat16)
        recon = jnp.einsum("scr,srt->sct", basis, coeff, preferred_element_type=jnp.float32)
        resid = slab_rows.astype(jnp.float32) - recon
        energy_term = jnp.sum(resid * resid, axis=2)
        gram_term = jnp.einsum("srt,sqt->srq", coeff, coeff, preferred_element_type=jnp.float32)
        gram_total, energy_total = lax.psum((gram_term, energy_term), "seq")
        gram_list.append(gram_total / tokens)
        energy_list.append(energy_total / tokens)
        block_list.append(coeff.reshape(2 * rank, blk_dev, blk_rows).transpose(1, 0, 2))
    grams = jnp.stack(gram_list)
    energies = jnp.stack(energy_list)
    unit_count = layers * blk_dev
    units = jnp.stack(block_list).reshape(unit_count, 2 * rank * blk_rows)
    slot_vals = owner_slots.reshape(unit_count)
    one_hot = (slot_vals[:, None] == jnp.arange(CAP, dtype=jnp.int32)[None, :]).astype(jnp.bfloat16)
    outgoing = jnp.einsum("us,uf->sf", one_hot, units, preferred_element_type=jnp.float32).astype(
        jnp.bfloat16
    )
    outgoing = outgoing.reshape(REACH, OWNER_SLOT_LIMIT, 2 * rank, blk_rows)
    arrived = [outgoing[0]]
    for offset in range(1, REACH):
        arrived.append(from_behind(outgoing[offset], "seq", offset))
    buffer_all = jnp.stack(arrived)
    received = buffer_all.reshape(REACH * OWNER_SLOT_LIMIT, 2 * rank, blk_rows)
    return (received, grams, energies)


def solution(mesh):
    in_specs = (P(None, "seq", "groups"), P(), P(None, ("groups", "seq")))
    out_specs = (
        P(("groups", "seq"), None, None),
        P("groups", None, None, None),
        P("groups", None, None),
    )
    return jax.shard_map(
        per_device, mesh=mesh, in_specs=in_specs, out_specs=out_specs, check_vma=False
    )
```

profile of v0, /device:TPU:0, one launch (start us, length us, event | category | flops | bytes accessed | tf_op | source)
XLA Modules:
  0.0 329.7 jit_solution(11468838820563559150)
XLA Ops:
  7.2 7.2 %copy.39 = bf16[3,128,4096]{1,0,2:T(4,128)(2,1)} copy(bf16[3,128,4096]{2,1,0:T(8,128)(2,1)} %param.3) | data formatting | bytes 6291456 | tf_op args[0]
  14.4 7.5 %all-to-all-start = ((bf16[3,128,4096]{1,0,2:T(4,128)(2,1)}), bf16[3,128,4096]{1,0,2:T(4,128)(2,1)}, u32[]{:S(2)}, u32[]{:S(2)}) async-start(bf16[3,128,4096]{1,0,2:T(4,128)(2,1)} %copy.39), calls=%async_computation | async-start | bytes 8388608 | tf_op jit(solution)/shard_map/all_to_all | solution.py:26
  22.2 77.4 %all-to-all-done = bf16[3,128,4096]{1,0,2:T(4,128)(2,1)} async-done(((bf16[3,128,4096]{1,0,2:T(4,128)(2,1)}), bf16[3,128,4096]{1,0,2:T(4,128)(2,1)}, u32[]{:S(2)}, u32[]{:S(2)}) %all-to-all-start) | async-done | bytes 3145760 | tf_op jit(solution)/shard_map/all_to_all | solution.py:26
  99.6 5.5 %copy.40 = bf16[3,128,16,256]{3,1,2,0:T(8,128)(2,1)S(1)} copy(bf16[3,128,16,256]{1,0,3,2:T(4,128)(2,1)} %bitcast.1) | data formatting | bytes 6291456 | tf_op jit(solution)/shard_map/all_to_all | solution.py:26
  105.2 1.6 fusion.21
  106.8 1.0 copy-done.4
  109.5 1.8 convolution_convert_fusion.1
  111.3 1.9 fusion.1
  113.3 1.7 convolution_convert_fusion.3
  115.0 1.8 fusion.5
  116.9 1.1 fusion.22
  118.0 1.1 fusion.23
  119.0 1.1 fusion.24
  120.3 0.9 convolution_convert_fusion
  121.2 1.5 slice_bitcast_fusion
  123.5 0.8 collective-permute-start
  124.4 6.2 %collective-permute-start.1 = (bf16[2,512,128]{2,1,0:T(8,128)(2,1)S(1)}, bf16[2,512,128]{2,1,0:T(8,128)(2,1)S(1)}, u32[]{:S(2)}, u32[]{:S(2)}) collective-permute-start(bf16[2,512,128]{2,1,0:T(8,128)(2,1)S(1)} %bitcast.153), channel_id=1, source_target_pairs={{14,0},{15,1},{0,2},{1,3},{2,4},{3,5},{4,6},{5,7},{6,8},{7,9},{8,1... | collective-permute-start | bytes 786440 | tf_op jit(solution)/shard_map/ppermute | solution.py:14
  130.7 12.0 %collective-permute-start.2 = (bf16[2,512,128]{2,1,0:T(8,128)(2,1)S(1)}, bf16[2,512,128]{2,1,0:T(8,128)(2,1)S(1)}, u32[]{:S(2)}, u32[]{:S(2)}) collective-permute-start(bf16[2,512,128]{2,1,0:T(8,128)(2,1)S(1)} %bitcast.152), channel_id=1, source_target_pairs={{13,0},{14,1},{15,2},{0,3},{1,4},{2,5},{3,6},{4,7},{5,8},{6,9},{7,... | collective-permute-start | bytes 786440 | tf_op jit(solution)/shard_map/ppermute | solution.py:14
  143.6 75.5 %all-reduce = (f32[2,1024]{1,0:T(2,128)S(1)}, f32[2,1024]{1,0:T(2,128)S(1)}, f32[2,1024]{1,0:T(2,128)S(1)}) all-reduce(f32[2,1024]{1,0:T(2,128)S(1)} %fusion.1, f32[2,1024]{1,0:T(2,128)S(1)} %fusion.3, f32[2,1024]{1,0:T(2,128)S(1)} %fusion.5), channel_id=1, replica_groups=mesh['groups'=2,'seq'=16] {'seq'}, use_global_device_ids=true, to_apply=%region_8.0 | all-reduce | flops 6144 | bytes 49152 | tf_op jit(solution)/shard_map/psum | solution.py:41
  223.6 16.2 %collective-permute-done.5 = bf16[2,512,128]{2,1,0:T(8,128)(2,1)S(1)} collective-permute-done((bf16[2,512,128]{2,1,0:T(8,128)(2,1)S(1)}, bf16[2,512,128]{2,1,0:T(8,128)(2,1)S(1)}, u32[]{:S(2)}, u32[]{:S(2)}) %collective-permute-start.5) | collective-permute-done | bytes 262176 | tf_op jit(solution)/shard_map/ppermute | solution.py:14
  241.2 78.0 %all-reduce.4.cloned.1.call-done = (f32[2,256,256]{2,1,0:T(8,128)}, f32[2,256,256]{2,1,0:T(8,128)}, f32[2,256,256]{2,1,0:T(8,128)}) async-done(((f32[2,256,256]{2,1,0:T(8,128)}, f32[2,256,256]{2,1,0:T(8,128)}, f32[2,256,256]{2,1,0:T(8,128)}), (f32[2,256,256]{2,1,0:T(8,128)}, f32[2,256,256]{2,1,0:T(8,128)}, f32[2,256,256]{2,1,0:T(8,128)})) %all-reduce.4.cloned.1.call-update) | async-done | bytes 1572880 | tf_op jit(solution)/shard_map/psum | solution.py:41
  319.2 1.1 multiply_bitcast_fusion.2
  320.3 1.3 multiply_bitcast_fusion
  321.6 1.2 pad_maximum_fusion
  (49 shorter events, 10.0 us)
Async XLA Ops:
  14.4 7.6 %copy-start.3 = (s32[3,2]{0,1:T(2,128)S(1)}, s32[3,2]{0,1:T(2,128)}, u32[]{:S(2)}) copy-start(s32[3,2]{0,1:T(2,128)} %param.5) | copy-start | bytes 76
  14.4 85.2 %all-to-all-start = ((bf16[3,128,4096]{1,0,2:T(4,128)(2,1)}), bf16[3,128,4096]{1,0,2:T(4,128)(2,1)}, u32[]{:S(2)}, u32[]{:S(2)}) async-start(bf16[3,128,4096]{1,0,2:T(4,128)(2,1)} %copy.39), calls=%async_computation | async-start | bytes 8388608 | tf_op jit(solution)/shard_map/all_to_all | solution.py:26
  22.0 297.3 %all-reduce.4.cloned.1.call-start = ((), (), s32[]{:S(2)}) async-start(), calls=%async_computation.1 | async-start | bytes 3145728 | tf_op jit(solution)/shard_map/psum | solution.py:41
  105.1 2.6 copy-start.4
  108.3 1.2 copy-start.1
  109.0 2.3 copy-start.2
  111.3 2.0 copy-start
  123.5 96.4 %collective-permute-start = (bf16[2,512,128]{2,1,0:T(8,128)(2,1)S(1)}, bf16[2,512,128]{2,1,0:T(8,128)(2,1)S(1)}, u32[]{:S(2)}, u32[]{:S(2)}) collective-permute-start(bf16[2,512,128]{2,1,0:T(8,128)(2,1)S(1)} %bitcast.154), channel_id=1, source_target_pairs={{15,0},{0,1},{1,2},{2,3},{3,4},{4,5},{5,6},{6,7},{7,8},{8,9},{9,10... | collective-permute-start | bytes 786440 | tf_op jit(solution)/shard_map/ppermute | solution.py:14
  124.4 96.3 %collective-permute-start.1 = (bf16[2,512,128]{2,1,0:T(8,128)(2,1)S(1)}, bf16[2,512,128]{2,1,0:T(8,128)(2,1)S(1)}, u32[]{:S(2)}, u32[]{:S(2)}) collective-permute-start(bf16[2,512,128]{2,1,0:T(8,128)(2,1)S(1)} %bitcast.153), channel_id=1, source_target_pairs={{14,0},{15,1},{0,2},{1,3},{2,4},{3,5},{4,6},{5,7},{6,8},{7,9},{8,1... | collective-permute-start | bytes 786440 | tf_op jit(solution)/shard_map/ppermute | solution.py:14
  130.7 90.7 %collective-permute-start.2 = (bf16[2,512,128]{2,1,0:T(8,128)(2,1)S(1)}, bf16[2,512,128]{2,1,0:T(8,128)(2,1)S(1)}, u32[]{:S(2)}, u32[]{:S(2)}) collective-permute-start(bf16[2,512,128]{2,1,0:T(8,128)(2,1)S(1)} %bitcast.152), channel_id=1, source_target_pairs={{13,0},{14,1},{15,2},{0,3},{1,4},{2,5},{3,6},{4,7},{5,8},{6,9},{7,... | collective-permute-start | bytes 786440 | tf_op jit(solution)/shard_map/ppermute | solution.py:14
  142.7 79.4 %collective-permute-start.3 = (bf16[2,512,128]{2,1,0:T(8,128)(2,1)S(1)}, bf16[2,512,128]{2,1,0:T(8,128)(2,1)S(1)}, u32[]{:S(2)}, u32[]{:S(2)}) collective-permute-start(bf16[2,512,128]{2,1,0:T(8,128)(2,1)S(1)} %bitcast.151), channel_id=1, source_target_pairs={{12,0},{13,1},{14,2},{15,3},{0,4},{1,5},{2,6},{3,7},{4,8},{5,9},{6... | collective-permute-start | bytes 786440 | tf_op jit(solution)/shard_map/ppermute | solution.py:14
  143.5 79.4 %collective-permute-start.4 = (bf16[2,512,128]{2,1,0:T(8,128)(2,1)S(1)}, bf16[2,512,128]{2,1,0:T(8,128)(2,1)S(1)}, u32[]{:S(2)}, u32[]{:S(2)}) collective-permute-start(bf16[2,512,128]{2,1,0:T(8,128)(2,1)S(1)} %bitcast.150), channel_id=1, source_target_pairs={{11,0},{12,1},{13,2},{14,3},{15,4},{0,5},{1,6},{2,7},{3,8},{4,9},{... | collective-permute-start | bytes 786440 | tf_op jit(solution)/shard_map/ppermute | solution.py:14
  219.9 19.9 %collective-permute-start.5 = (bf16[2,512,128]{2,1,0:T(8,128)(2,1)S(1)}, bf16[2,512,128]{2,1,0:T(8,128)(2,1)S(1)}, u32[]{:S(2)}, u32[]{:S(2)}) collective-permute-start(bf16[2,512,128]{2,1,0:T(8,128)(2,1)S(1)} %bitcast.156), channel_id=1, source_target_pairs={{10,0},{11,1},{12,2},{13,3},{14,4},{15,5},{0,6},{1,7},{2,8},{3,9},... | collective-permute-start | bytes 786440 | tf_op jit(solution)/shard_map/ppermute | solution.py:14
  220.7 19.8 %collective-permute-start.6 = (bf16[2,512,128]{2,1,0:T(8,128)(2,1)S(1)}, bf16[2,512,128]{2,1,0:T(8,128)(2,1)S(1)}, u32[]{:S(2)}, u32[]{:S(2)}) collective-permute-start(bf16[2,512,128]{2,1,0:T(8,128)(2,1)S(1)} %bitcast.155), channel_id=1, source_target_pairs={{9,0},{10,1},{11,2},{12,3},{13,4},{14,5},{15,6},{0,7},{1,8},{2,9},... | collective-permute-start | bytes 786440 | tf_op jit(solution)/shard_map/ppermute | solution.py:14
Sparse Core Ops, SparseCore 0:
  220.0 99.1 all-reduce.3
where the time goes:
time: 330 us
  waiting for transfers between devices  172 us (52%)
  blocking collectives  75.5 us (23%)
  starting transfers between devices  27.6 us (8%)
  local copies, waits for them, and re-layouts  24 us (7%)
  between operations  14.3 us (4%)
  matrix products  12.3 us (4%)
  other arithmetic  4.34 us (1%)
    psum x1, waiting for transfers between devices, per_device(): gram_total, energy_total = lax.psum((gram_term, energy_term), 'seq')  78 us
    all_to_all x1, waiting for transfers between devices, per_device(): lax.all_to_all(key_values, 'seq', split_axis=2, concat_axis=1, tiled=True)  77.4 us
    psum x1, blocking collectives, per_device(): gram_total, energy_total = lax.psum((gram_term, energy_term), 'seq')  75.5 us
    ppermute x7, starting transfers between devices, from_behind(): return lax.ppermute(block, axis, route)  20 us
    ppermute x7, waiting for transfers between devices, from_behind(): return lax.ppermute(block, axis, route)  16.2 us
    unnamed x27, local copies, waits for them, and re-layouts  15.8 us
    all_to_all x1, starting transfers between devices, per_device(): lax.all_to_all(key_values, 'seq', split_axis=2, concat_axis=1, tiled=True)  7.54 us
  transfers between devices with their start and end apart: 9, of which 3 were waited for; matrix products, arithmetic and copies ran while one was open for 2% of the time, Pallas kernels for 0%

commit v1 on v0

--- a/solution.py
+++ b/solution.py
@@ -6,6 +6,18 @@
 REACH = 8
 OWNER_SLOT_LIMIT = 2
 CAP = 16
+
+
+def exchange_directly(x, axis, split, join):
+    ways, here = (lax.axis_size(axis), lax.axis_index(axis))
+    width = x.shape[split] // ways
+    turned = jnp.roll(x, -here * width, axis=split)
+    got = [lax.slice_in_dim(turned, 0, width, axis=split)]
+    for far in range(1, ways):
+        sent = lax.slice_in_dim(turned, far * width, (far + 1) * width, axis=split)
+        got.append(lax.ppermute(sent, axis, [(d, (d + far) % ways) for d in range(ways)]))
+    line = jnp.concatenate(got[::-1], axis=join)
+    return jnp.roll(line, (here + 1) * got[0].shape[join], axis=join)
 
 
 def from_behind(block, axis, distance):
@@ -23,7 +35,7 @@
     tokens = tok_dev * dev_count
     blk_dev = owner_slots.shape[1]
     blk_rows = tok_dev // blk_dev
-    whole = lax.all_to_all(key_values, "seq", split_axis=2, concat_axis=1, tiled=True)
+    whole = exchange_directly(key_values, "seq", 2, 1)
     gram_list = []
     energy_list = []
     block_list = []

time: 330 us -> 314 us (0.952)
  waiting for transfers between devices: 172 us -> 144 us
  starting transfers between devices: 27.6 us -> 33.3 us
  local copies, waits for them, and re-layouts: 24 us -> 19.5 us
  other arithmetic: 4.34 us -> 8.75 us
    all_to_all x1 -> x0, waiting for transfers between devices: 77.4 us -> none  [per_device(): lax.all_to_all(key_values, 'seq', split_axis=2, concat_axis=1, tiled=True)]
    ppermute x0 -> x15, waiting for transfers between devices: none -> 49.3 us  [exchange_directly(): lax.ppermute(sent, axis, [(d, (d + far) % ways) for d in range(ways)])]
    ppermute x0 -> x15, starting transfers between devices: none -> 29.7 us  [exchange_directly(): lax.ppermute(sent, axis, [(d, (d + far) % ways) for d in range(ways)])]
    ppermute x7, starting transfers between devices: 20 us -> 3.5 us  [from_behind(): return lax.ppermute(block, axis, route)]
    all_to_all x1 -> x0, starting transfers between devices: 7.54 us -> none  [per_device(): lax.all_to_all(key_values, 'seq', split_axis=2, concat_axis=1, tiled=True)]
    all_to_all x1 -> x0, local copies, waits for them, and re-layouts: 5.5 us -> none  [per_device(): lax.all_to_all(key_values, 'seq', split_axis=2, concat_axis=1, tiled=True)]
    unnamed x27 -> x51, local copies, waits for them, and re-layouts: 15.8 us -> 13 us
  transfers between devices with their start and end apart: 9 -> 23, of which waited for: 3 -> 12; matrix products, arithmetic and copies ran while one was open for 2% -> 3% of each run, Pallas kernels for 0% -> 0%
where the time goes in v1:
time: 314 us; the launch traced here: 313 us
  waiting for transfers between devices  144 us (46%)
  blocking collectives  78.2 us (25%)
  starting transfers between devices  33.3 us (11%)
  local copies, waits for them, and re-layouts  19.5 us (6%)
  matrix products  15 us (5%)
  between operations  14.6 us (5%)
  other arithmetic  8.75 us (3%)
    psum x1, waiting for transfers between devices, per_device(): gram_total, energy_total = lax.psum((gram_term, energy_term), 'seq')  78.2 us
    psum x1, blocking collectives, per_device(): gram_total, energy_total = lax.psum((gram_term, energy_term), 'seq')  78.2 us
    ppermute x15, waiting for transfers between devices, exchange_directly(): lax.ppermute(sent, axis, [(d, (d + far) % ways) for d in range(ways)])  49.3 us
    ppermute x15, starting transfers between devices, exchange_directly(): lax.ppermute(sent, axis, [(d, (d + far) % ways) for d in range(ways)])  29.7 us
    ppermute x7, waiting for transfers between devices, from_behind(): return lax.ppermute(block, axis, route)  16.1 us
    unnamed x51, local copies, waits for them, and re-layouts  13 us
  transfers between devices with their start and end apart: 23, of which 12 were waited for; matrix products, arithmetic and copies ran while one was open for 3% of the time, Pallas kernels for 0%

profile of v1, /device:TPU:0, one launch (start us, length us, event | category | flops | bytes accessed | tf_op | source)
XLA Modules:
  0.0 313.0 jit_solution(9255597524868453331)
XLA Ops:
  7.2 3.2 %fusion = bf16[3,128,4096]{2,1,0:T(8,128)(2,1)S(1)} fusion(s32[]{:T(128)S(6)} %select_n.24, bf16[3,128,4096]{2,1,0:T(8,128)(2,1)} %param.3), kind=kLoop, calls=%fused_computation.3 | loop fusion | flops 6291456 | bytes 6291460 | tf_op jit(solution)/shard_map/jit(_roll_dynamic)/concatenate | solution.py:14
  10.5 1.6 fusion.25
  12.1 5.5 %collective-permute-start = (bf16[3,128,256]{2,1,0:T(8,128)(2,1)}, bf16[3,128,256]{2,1,0:T(8,128)(2,1)S(1)}, u32[]{:S(2)}, u32[]{:S(2)}) collective-permute-start(bf16[3,128,256]{2,1,0:T(8,128)(2,1)} %get-tuple-element.26), channel_id=1, source_target_pairs={{0,15},{1,0},{2,1},{3,2},{4,3},{5,4},{6,5},{7,6},{8,7},{9,8},{10,9... | collective-permute-start | bytes 589832 | tf_op jit(solution)/shard_map/ppermute | solution.py:18
  19.0 4.2 %collective-permute-done = bf16[3,128,256]{2,1,0:T(8,128)(2,1)S(1)} collective-permute-done((bf16[3,128,256]{2,1,0:T(8,128)(2,1)}, bf16[3,128,256]{2,1,0:T(8,128)(2,1)S(1)}, u32[]{:S(2)}, u32[]{:S(2)}) %collective-permute-start) | collective-permute-done | bytes 196640 | tf_op jit(solution)/shard_map/ppermute | solution.py:18
  23.5 3.9 %collective-permute-done.1 = bf16[3,128,256]{2,1,0:T(8,128)(2,1)S(1)} collective-permute-done((bf16[3,128,256]{2,1,0:T(8,128)(2,1)}, bf16[3,128,256]{2,1,0:T(8,128)(2,1)S(1)}, u32[]{:S(2)}, u32[]{:S(2)}) %collective-permute-start.1) | collective-permute-done | bytes 196640 | tf_op jit(solution)/shard_map/ppermute | solution.py:18
  27.4 4.2 %collective-permute-done.2 = bf16[3,128,256]{2,1,0:T(8,128)(2,1)} collective-permute-done((bf16[3,128,256]{2,1,0:T(8,128)(2,1)}, bf16[3,128,256]{2,1,0:T(8,128)(2,1)}, u32[]{:S(2)}, u32[]{:S(2)}) %collective-permute-start.2) | collective-permute-done | bytes 196640 | tf_op jit(solution)/shard_map/ppermute | solution.py:18
  32.5 3.3 %collective-permute-done.3 = bf16[3,128,256]{2,1,0:T(8,128)(2,1)} collective-permute-done((bf16[3,128,256]{2,1,0:T(8,128)(2,1)}, bf16[3,128,256]{2,1,0:T(8,128)(2,1)}, u32[]{:S(2)}, u32[]{:S(2)}) %collective-permute-start.3) | collective-permute-done | bytes 196640 | tf_op jit(solution)/shard_map/ppermute | solution.py:18
  36.7 3.3 %collective-permute-done.4 = bf16[3,128,256]{2,1,0:T(8,128)(2,1)} collective-permute-done((bf16[3,128,256]{2,1,0:T(8,128)(2,1)}, bf16[3,128,256]{2,1,0:T(8,128)(2,1)}, u32[]{:S(2)}, u32[]{:S(2)}) %collective-permute-start.4) | collective-permute-done | bytes 196640 | tf_op jit(solution)/shard_map/ppermute | solution.py:18
  40.9 3.3 %collective-permute-done.5 = bf16[3,128,256]{2,1,0:T(8,128)(2,1)S(1)} collective-permute-done((bf16[3,128,256]{2,1,0:T(8,128)(2,1)}, bf16[3,128,256]{2,1,0:T(8,128)(2,1)S(1)}, u32[]{:S(2)}, u32[]{:S(2)}) %collective-permute-start.5) | collective-permute-done | bytes 196640 | tf_op jit(solution)/shard_map/ppermute | solution.py:18
  44.2 13.9 %collective-permute-start.10 = (bf16[3,128,256]{2,1,0:T(8,128)(2,1)}, bf16[3,128,256]{2,1,0:T(8,128)(2,1)S(1)}, u32[]{:S(2)}, u32[]{:S(2)}) collective-permute-start(bf16[3,128,256]{2,1,0:T(8,128)(2,1)} %get-tuple-element.16), channel_id=1, source_target_pairs={{0,5},{1,6},{2,7},{3,8},{4,9},{5,10},{6,11},{7,12},{8,13},{9,14},{... | collective-permute-start | bytes 589832 | tf_op jit(solution)/shard_map/ppermute | solution.py:18
  58.2 8.5 %collective-permute-start.11 = (bf16[3,128,256]{2,1,0:T(8,128)(2,1)}, bf16[3,128,256]{2,1,0:T(8,128)(2,1)S(1)}, u32[]{:S(2)}, u32[]{:S(2)}) collective-permute-start(bf16[3,128,256]{2,1,0:T(8,128)(2,1)} %get-tuple-element.15), channel_id=1, source_target_pairs={{0,4},{1,5},{2,6},{3,7},{4,8},{5,9},{6,10},{7,11},{8,12},{9,13},{1... | collective-permute-start | bytes 589832 | tf_op jit(solution)/shard_map/ppermute | solution.py:18
  66.7 17.2 %collective-permute-done.7 = bf16[3,128,256]{2,1,0:T(8,128)(2,1)S(1)} collective-permute-done((bf16[3,128,256]{2,1,0:T(8,128)(2,1)}, bf16[3,128,256]{2,1,0:T(8,128)(2,1)S(1)}, u32[]{:S(2)}, u32[]{:S(2)}) %collective-permute-start.7) | collective-permute-done | bytes 196640 | tf_op jit(solution)/shard_map/ppermute | solution.py:18
  84.4 6.6 %collective-permute-done.12 = bf16[3,128,256]{2,1,0:T(8,128)(2,1)S(1)} collective-permute-done((bf16[3,128,256]{2,1,0:T(8,128)(2,1)}, bf16[3,128,256]{2,1,0:T(8,128)(2,1)S(1)}, u32[]{:S(2)}, u32[]{:S(2)}) %collective-permute-start.12) | collective-permute-done | bytes 196640 | tf_op jit(solution)/shard_map/ppermute | solution.py:18
  91.0 3.4 %collective-permute-done.13 = bf16[3,128,256]{2,1,0:T(8,128)(2,1)S(1)} collective-permute-done((bf16[3,128,256]{2,1,0:T(8,128)(2,1)}, bf16[3,128,256]{2,1,0:T(8,128)(2,1)S(1)}, u32[]{:S(2)}, u32[]{:S(2)}) %collective-permute-start.13) | collective-permute-done | bytes 196640 | tf_op jit(solution)/shard_map/ppermute | solution.py:18
  99.2 1.7 convolution_convert_fusion.3
  102.2 1.7 convolution_convert_fusion.2
  104.5 1.8 convolution_convert_fusion.1
  107.4 2.0 fusion.6
  110.6 1.7 fusion.4
  113.4 1.7 fusion.2
  121.3 1.8 collective-permute-start.18
  124.1 78.2 %all-reduce = (f32[2,1024]{1,0:T(2,128)S(1)}, f32[2,1024]{1,0:T(2,128)S(1)}, f32[2,1024]{1,0:T(2,128)S(1)}) all-reduce(f32[2,1024]{1,0:T(2,128)S(1)} %fusion.2, f32[2,1024]{1,0:T(2,128)S(1)} %fusion.4, f32[2,1024]{1,0:T(2,128)S(1)} %fusion.6), channel_id=1, replica_groups=mesh['groups'=2,'seq'=16] {'seq'}, use_global_device_ids=true, to_apply=%region_8.9 | all-reduce | flops 6144 | bytes 49152 | tf_op jit(solution)/shard_map/psum | solution.py:53
  206.7 16.1 %collective-permute-done.20 = bf16[2,512,128]{2,1,0:T(8,128)(2,1)S(1)} collective-permute-done((bf16[2,512,128]{2,1,0:T(8,128)(2,1)S(1)}, bf16[2,512,128]{2,1,0:T(8,128)(2,1)S(1)}, u32[]{:S(2)}, u32[]{:S(2)}) %collective-permute-start.20) | collective-permute-done | bytes 262176 | tf_op jit(solution)/shard_map/ppermute | solution.py:26
  224.2 78.2 %all-reduce.4.cloned.1.call-done = (f32[2,256,256]{2,1,0:T(8,128)}, f32[2,256,256]{2,1,0:T(8,128)}, f32[2,256,256]{2,1,0:T(8,128)}) async-done(((f32[2,256,256]{2,1,0:T(8,128)}, f32[2,256,256]{2,1,0:T(8,128)}, f32[2,256,256]{2,1,0:T(8,128)}), (f32[2,256,256]{2,1,0:T(8,128)}, f32[2,256,256]{2,1,0:T(8,128)}, f32[2,256,256]{2,1,0:T(8,128)})) %all-reduce.4.cloned.1.call-update) | async-done | bytes 1572880 | tf_op jit(solution)/shard_map/psum | solution.py:53
  (108 shorter events, 31.3 us)
Async XLA Ops:
  7.2 11.6 %copy-start.1 = (s32[3,2]{0,1:T(2,128)S(1)}, s32[3,2]{0,1:T(2,128)}, u32[]{:S(2)}) copy-start(s32[3,2]{0,1:T(2,128)} %param.5) | copy-start | bytes 76
  7.2 295.3 %all-reduce.4.cloned.1.call-start = ((), (), s32[]{:S(2)}) async-start(), calls=%async_computation | async-start | bytes 3145728 | tf_op jit(solution)/shard_map/psum | solution.py:53
  12.1 11.1 %collective-permute-start = (bf16[3,128,256]{2,1,0:T(8,128)(2,1)}, bf16[3,128,256]{2,1,0:T(8,128)(2,1)S(1)}, u32[]{:S(2)}, u32[]{:S(2)}) collective-permute-start(bf16[3,128,256]{2,1,0:T(8,128)(2,1)} %get-tuple-element.26), channel_id=1, source_target_pairs={{0,15},{1,0},{2,1},{3,2},{4,3},{5,4},{6,5},{7,6},{8,7},{9,8},{10,9... | collective-permute-start | bytes 589832 | tf_op jit(solution)/shard_map/ppermute | solution.py:18
  17.6 9.8 %collective-permute-start.1 = (bf16[3,128,256]{2,1,0:T(8,128)(2,1)}, bf16[3,128,256]{2,1,0:T(8,128)(2,1)S(1)}, u32[]{:S(2)}, u32[]{:S(2)}) collective-permute-start(bf16[3,128,256]{2,1,0:T(8,128)(2,1)} %get-tuple-element.25), channel_id=1, source_target_pairs={{0,14},{1,15},{2,0},{3,1},{4,2},{5,3},{6,4},{7,5},{8,6},{9,7},{10,... | collective-permute-start | bytes 589832 | tf_op jit(solution)/shard_map/ppermute | solution.py:18
  18.1 13.5 %collective-permute-start.2 = (bf16[3,128,256]{2,1,0:T(8,128)(2,1)}, bf16[3,128,256]{2,1,0:T(8,128)(2,1)}, u32[]{:S(2)}, u32[]{:S(2)}) collective-permute-start(bf16[3,128,256]{2,1,0:T(8,128)(2,1)} %get-tuple-element.24), channel_id=1, source_target_pairs={{0,13},{1,14},{2,15},{3,0},{4,1},{5,2},{6,3},{7,4},{8,5},{9,6},{10... | collective-permute-start | bytes 589832 | tf_op jit(solution)/shard_map/ppermute | solution.py:18
  18.4 17.4 %collective-permute-start.3 = (bf16[3,128,256]{2,1,0:T(8,128)(2,1)}, bf16[3,128,256]{2,1,0:T(8,128)(2,1)}, u32[]{:S(2)}, u32[]{:S(2)}) collective-permute-start(bf16[3,128,256]{2,1,0:T(8,128)(2,1)} %get-tuple-element.23), channel_id=1, source_target_pairs={{0,12},{1,13},{2,14},{3,15},{4,0},{5,1},{6,2},{7,3},{8,4},{9,5},{1... | collective-permute-start | bytes 589832 | tf_op jit(solution)/shard_map/ppermute | solution.py:18
  18.8 21.2 %collective-permute-start.4 = (bf16[3,128,256]{2,1,0:T(8,128)(2,1)}, bf16[3,128,256]{2,1,0:T(8,128)(2,1)}, u32[]{:S(2)}, u32[]{:S(2)}) collective-permute-start(bf16[3,128,256]{2,1,0:T(8,128)(2,1)} %get-tuple-element.22), channel_id=1, source_target_pairs={{0,11},{1,12},{2,13},{3,14},{4,15},{5,0},{6,1},{7,2},{8,3},{9,4},{... | collective-permute-start | bytes 589832 | tf_op jit(solution)/shard_map/ppermute | solution.py:18
  23.1 21.1 %collective-permute-start.5 = (bf16[3,128,256]{2,1,0:T(8,128)(2,1)}, bf16[3,128,256]{2,1,0:T(8,128)(2,1)S(1)}, u32[]{:S(2)}, u32[]{:S(2)}) collective-permute-start(bf16[3,128,256]{2,1,0:T(8,128)(2,1)} %get-tuple-element.21), channel_id=1, source_target_pairs={{0,10},{1,11},{2,12},{3,13},{4,14},{5,15},{6,0},{7,1},{8,2},{9,3},... | collective-permute-start | bytes 589832 | tf_op jit(solution)/shard_map/ppermute | solution.py:18
  27.4 30.8 %collective-permute-start.6 = (bf16[3,128,256]{2,1,0:T(8,128)(2,1)}, bf16[3,128,256]{2,1,0:T(8,128)(2,1)S(1)}, u32[]{:S(2)}, u32[]{:S(2)}) collective-permute-start(bf16[3,128,256]{2,1,0:T(8,128)(2,1)} %get-tuple-element.20), channel_id=1, source_target_pairs={{0,9},{1,10},{2,11},{3,12},{4,13},{5,14},{6,15},{7,0},{8,1},{9,2},... | collective-permute-start | bytes 589832 | tf_op jit(solution)/shard_map/ppermute | solution.py:18
  31.6 52.3 %collective-permute-start.7 = (bf16[3,128,256]{2,1,0:T(8,128)(2,1)}, bf16[3,128,256]{2,1,0:T(8,128)(2,1)S(1)}, u32[]{:S(2)}, u32[]{:S(2)}) collective-permute-start(bf16[3,128,256]{2,1,0:T(8,128)(2,1)} %get-tuple-element.19), channel_id=1, source_target_pairs={{0,8},{1,9},{2,10},{3,11},{4,12},{5,13},{6,14},{7,15},{8,0},{9,1},... | collective-permute-start | bytes 589832 | tf_op jit(solution)/shard_map/ppermute | solution.py:18
  35.8 48.2 %collective-permute-start.8 = (bf16[3,128,256]{2,1,0:T(8,128)(2,1)}, bf16[3,128,256]{2,1,0:T(8,128)(2,1)S(1)}, u32[]{:S(2)}, u32[]{:S(2)}) collective-permute-start(bf16[3,128,256]{2,1,0:T(8,128)(2,1)} %get-tuple-element.18), channel_id=1, source_target_pairs={{0,7},{1,8},{2,9},{3,10},{4,11},{5,12},{6,13},{7,14},{8,15},{9,0},... | collective-permute-start | bytes 589832 | tf_op jit(solution)/shard_map/ppermute | solution.py:18
  40.0 44.0 %collective-permute-start.9 = (bf16[3,128,256]{2,1,0:T(8,128)(2,1)}, bf16[3,128,256]{2,1,0:T(8,128)(2,1)S(1)}, u32[]{:S(2)}, u32[]{:S(2)}) collective-permute-start(bf16[3,128,256]{2,1,0:T(8,128)(2,1)} %get-tuple-element.17), channel_id=1, source_target_pairs={{0,6},{1,7},{2,8},{3,9},{4,10},{5,11},{6,12},{7,13},{8,14},{9,15},... | collective-permute-start | bytes 589832 | tf_op jit(solution)/shard_map/ppermute | solution.py:18
  44.2 40.1 %collective-permute-start.10 = (bf16[3,128,256]{2,1,0:T(8,128)(2,1)}, bf16[3,128,256]{2,1,0:T(8,128)(2,1)S(1)}, u32[]{:S(2)}, u32[]{:S(2)}) collective-permute-start(bf16[3,128,256]{2,1,0:T(8,128)(2,1)} %get-tuple-element.16), channel_id=1, source_target_pairs={{0,5},{1,6},{2,7},{3,8},{4,9},{5,10},{6,11},{7,12},{8,13},{9,14},{... | collective-permute-start | bytes 589832 | tf_op jit(solution)/shard_map/ppermute | solution.py:18
  58.2 26.2 %collective-permute-start.11 = (bf16[3,128,256]{2,1,0:T(8,128)(2,1)}, bf16[3,128,256]{2,1,0:T(8,128)(2,1)S(1)}, u32[]{:S(2)}, u32[]{:S(2)}) collective-permute-start(bf16[3,128,256]{2,1,0:T(8,128)(2,1)} %get-tuple-element.15), channel_id=1, source_target_pairs={{0,4},{1,5},{2,6},{3,7},{4,8},{5,9},{6,10},{7,11},{8,12},{9,13},{1... | collective-permute-start | bytes 589832 | tf_op jit(solution)/shard_map/ppermute | solution.py:18
  83.9 7.1 %collective-permute-start.12 = (bf16[3,128,256]{2,1,0:T(8,128)(2,1)}, bf16[3,128,256]{2,1,0:T(8,128)(2,1)S(1)}, u32[]{:S(2)}, u32[]{:S(2)}) collective-permute-start(bf16[3,128,256]{2,1,0:T(8,128)(2,1)} %get-tuple-element.14), channel_id=1, source_target_pairs={{0,3},{1,4},{2,5},{3,6},{4,7},{5,8},{6,9},{7,10},{8,11},{9,12},{10... | collective-permute-start | bytes 589832 | tf_op jit(solution)/shard_map/ppermute | solution.py:18
  84.0 10.4 %collective-permute-start.13 = (bf16[3,128,256]{2,1,0:T(8,128)(2,1)}, bf16[3,128,256]{2,1,0:T(8,128)(2,1)S(1)}, u32[]{:S(2)}, u32[]{:S(2)}) collective-permute-start(bf16[3,128,256]{2,1,0:T(8,128)(2,1)} %get-tuple-element.13), channel_id=1, source_target_pairs={{0,2},{1,3},{2,4},{3,5},{4,6},{5,7},{6,8},{7,9},{8,10},{9,11},{10,... | collective-permute-start | bytes 589832 | tf_op jit(solution)/shard_map/ppermute | solution.py:18
  84.0 10.4 %collective-permute-start.14 = (bf16[3,128,256]{2,1,0:T(8,128)(2,1)}, bf16[3,128,256]{2,1,0:T(8,128)(2,1)S(1)}, u32[]{:S(2)}, u32[]{:S(2)}) collective-permute-start(bf16[3,128,256]{2,1,0:T(8,128)(2,1)} %get-tuple-element.12), channel_id=1, source_target_pairs={{0,1},{1,2},{2,3},{3,4},{4,5},{5,6},{6,7},{7,8},{8,9},{9,10},{10,1... | collective-permute-start | bytes 589832 | tf_op jit(solution)/shard_map/ppermute | solution.py:18
  120.4 82.6 %collective-permute-start.15 = (bf16[2,512,128]{2,1,0:T(8,128)(2,1)S(1)}, bf16[2,512,128]{2,1,0:T(8,128)(2,1)S(1)}, u32[]{:S(2)}, u32[]{:S(2)}) collective-permute-start(bf16[2,512,128]{2,1,0:T(8,128)(2,1)S(1)} %bitcast.155), channel_id=1, source_target_pairs={{15,0},{0,1},{1,2},{2,3},{3,4},{4,5},{5,6},{6,7},{7,8},{8,9},{9,10... | collective-permute-start | bytes 786440 | tf_op jit(solution)/shard_map/ppermute | solution.py:26
  120.5 83.3 %collective-permute-start.16 = (bf16[2,512,128]{2,1,0:T(8,128)(2,1)S(1)}, bf16[2,512,128]{2,1,0:T(8,128)(2,1)S(1)}, u32[]{:S(2)}, u32[]{:S(2)}) collective-permute-start(bf16[2,512,128]{2,1,0:T(8,128)(2,1)S(1)} %bitcast.154), channel_id=1, source_target_pairs={{14,0},{15,1},{0,2},{1,3},{2,4},{3,5},{4,6},{5,7},{6,8},{7,9},{8,1... | collective-permute-start | bytes 786440 | tf_op jit(solution)/shard_map/ppermute | solution.py:26
  120.7 83.9 %collective-permute-start.17 = (bf16[2,512,128]{2,1,0:T(8,128)(2,1)S(1)}, bf16[2,512,128]{2,1,0:T(8,128)(2,1)S(1)}, u32[]{:S(2)}, u32[]{:S(2)}) collective-permute-start(bf16[2,512,128]{2,1,0:T(8,128)(2,1)S(1)} %bitcast.153), channel_id=1, source_target_pairs={{13,0},{14,1},{15,2},{0,3},{1,4},{2,5},{3,6},{4,7},{5,8},{6,9},{7,... | collective-permute-start | bytes 786440 | tf_op jit(solution)/shard_map/ppermute | solution.py:26
  121.3 83.9 %collective-permute-start.18 = (bf16[2,512,128]{2,1,0:T(8,128)(2,1)S(1)}, bf16[2,512,128]{2,1,0:T(8,128)(2,1)S(1)}, u32[]{:S(2)}, u32[]{:S(2)}) collective-permute-start(bf16[2,512,128]{2,1,0:T(8,128)(2,1)S(1)} %bitcast.152), channel_id=1, source_target_pairs={{12,0},{13,1},{14,2},{15,3},{0,4},{1,5},{2,6},{3,7},{4,8},{5,9},{6... | collective-permute-start | bytes 786440 | tf_op jit(solution)/shard_map/ppermute | solution.py:26
  123.1 82.9 %collective-permute-start.19 = (bf16[2,512,128]{2,1,0:T(8,128)(2,1)S(1)}, bf16[2,512,128]{2,1,0:T(8,128)(2,1)S(1)}, u32[]{:S(2)}, u32[]{:S(2)}) collective-permute-start(bf16[2,512,128]{2,1,0:T(8,128)(2,1)S(1)} %bitcast.151), channel_id=1, source_target_pairs={{11,0},{12,1},{13,2},{14,3},{15,4},{0,5},{1,6},{2,7},{3,8},{4,9},{... | collective-permute-start | bytes 786440 | tf_op jit(solution)/shard_map/ppermute | solution.py:26
  203.0 19.8 %collective-permute-start.20 = (bf16[2,512,128]{2,1,0:T(8,128)(2,1)S(1)}, bf16[2,512,128]{2,1,0:T(8,128)(2,1)S(1)}, u32[]{:S(2)}, u32[]{:S(2)}) collective-permute-start(bf16[2,512,128]{2,1,0:T(8,128)(2,1)S(1)} %bitcast.157), channel_id=1, source_target_pairs={{10,0},{11,1},{12,2},{13,3},{14,4},{15,5},{0,6},{1,7},{2,8},{3,9},... | collective-permute-start | bytes 786440 | tf_op jit(solution)/shard_map/ppermute | solution.py:26
  203.8 19.7 %collective-permute-start.21 = (bf16[2,512,128]{2,1,0:T(8,128)(2,1)S(1)}, bf16[2,512,128]{2,1,0:T(8,128)(2,1)S(1)}, u32[]{:S(2)}, u32[]{:S(2)}) collective-permute-start(bf16[2,512,128]{2,1,0:T(8,128)(2,1)S(1)} %bitcast.156), channel_id=1, source_target_pairs={{9,0},{10,1},{11,2},{12,3},{13,4},{14,5},{15,6},{0,7},{1,8},{2,9},... | collective-permute-start | bytes 786440 | tf_op jit(solution)/shard_map/ppermute | solution.py:26
  (1 other events, 6.1 us)
Sparse Core Ops, SparseCore 0:
  203.1 99.3 all-reduce.3
